TPU v7x, 256 devices: a whole 4x4x8 slice. The times are simulated.
256 devices in a mesh: node: 64 (over y, z, core), feat: 4 (over x).
Axes of the slice: x: 4, y: 4, z: 8, core: 2. Of those that a mesh axis runs over, the one named last changes fastest.
Arguments:
- features: bfloat16 [32768, 128], P('node', 'feat'), may hold values from -10 to 10
- send_rows: int32 [64, 64, 64], P('node'), may hold values from 0 to 511
- send_count: int32 [64, 64], P('node'), may hold values from 1 to 64, 2048 in all within a row
- tile_src: int32 [256, 16], P('node'), may hold values from 0 to 35
- tile_val: bfloat16 [256, 16, 128, 128], P('node'), may hold values from 0 to 0.0009765625
- labels: int32 [32768], P('node'), may hold values from 0 to 171
- w_self1: bfloat16 [128, 1024], P('feat'), may hold values from -0.5 to 0.5
- w_neigh1: bfloat16 [128, 1024], P('feat'), may hold values from -0.5 to 0.5
- w_self2: bfloat16 [1024, 172], P('feat'), may hold values from -0.5 to 0.5
- w_neigh2: bfloat16 [1024, 172], P('feat'), may hold values from -0.1875 to 0.1875
Outputs:
- mean_loss: float32 [], replicated
- grad_self1: float32 [128, 1024], P('feat')
- grad_neigh1: float32 [128, 1024], P('feat')
- grad_self2: float32 [1024, 172], P('feat')
- grad_neigh2: float32 [1024, 172], P('feat')
Inputs may be any that keep to these rules, and one draw needn't show every extreme that they name: `send_rows`: row indices within the sending partition's 512 rows. Each row of send_count sums to 2048 and holds 64 at least once. `tile_src`: block numbers of the destination partition's source rows: numbers below 4 name its own rows, the others its halo slots.
All inputs are finite; a program needn't handle non-finite values.
Results may differ from a plain program's by a relative error of at most 0.00095.
The roundings to bfloat16 on the way count: a program that leaves them out, or rounds other values in their place, can miss the bound.
Values may be sent and summed in bfloat16 or wider, within the bound.
A program may use at most 64 MiB of HBM per device.

v0:
```python
import math
import jax
import jax.numpy as jnp
from jax import lax
from jax.sharding import PartitionSpec as P


def pack_rows(own_rows, send_rows, send_count):
    slot_total = send_rows.shape[2]
    picked = jnp.take(own_rows, send_rows[0].reshape(-1), axis=0)
    picked = picked.reshape(send_rows.shape[1], slot_total, own_rows.shape[1])
    in_use = jnp.arange(slot_total, dtype=jnp.int32)[None, :] < send_count[0][:, None]
    return jnp.where(in_use[:, :, None], picked, jnp.zeros_like(picked))


def aggregate(own_rows, arrived, tile_src, tile_val):
    col_count = own_rows.shape[1]
    blocks = jnp.concatenate([own_rows, arrived], axis=0).reshape(-1, 128, col_count)
    chosen = jnp.take(blocks, tile_src, axis=0)
    summed = jnp.einsum("bkij,bkjh->bih", tile_val, chosen, preferred_element_type=jnp.float32)
    return summed.reshape(own_rows.shape[0], col_count).astype(jnp.bfloat16)


def spread_back(grads, tile_src, tile_val, src_total):
    col_count = grads.shape[1]
    per_tile = jnp.einsum(
        "bkij,bih->bkjh",
        tile_val,
        grads.reshape(-1, 128, col_count),
        preferred_element_type=jnp.float32,
    )
    one_hot = (
        tile_src.reshape(-1)[None, :] == jnp.arange(src_total // 128, dtype=jnp.int32)[:, None]
    ).astype(jnp.float32)
    landed = jnp.dot(
        one_hot,
        per_tile.reshape(one_hot.shape[1], -1),
        precision=lax.Precision.HIGHEST,
        preferred_element_type=jnp.float32,
    )
    return landed.reshape(src_total, col_count)


def cross_entropy(logits, labels, grad_scale):
    row_max = jnp.max(logits, axis=1, keepdims=True)
    shifted = logits - row_max
    total_exp = jnp.sum(jnp.exp(shifted), axis=1, keepdims=True)
    classes = jnp.arange(logits.shape[1], dtype=jnp.int32)
    target = (labels[:, None] == classes[None, :]).astype(jnp.float32)
    row_loss = jnp.log(total_exp)[:, 0] - jnp.sum(shifted * target, axis=1)
    grads = ((jnp.exp(shifted) / total_exp - target) * grad_scale).astype(jnp.bfloat16)
    return (row_loss, grads)


def shards(
    features,
    send_rows,
    send_count,
    tile_src,
    tile_val,
    labels,
    w_self1,
    w_neigh1,
    w_self2,
    w_neigh2,
):
    node_count = lax.axis_size("node")
    own_count = features.shape[0]
    slot_total = send_rows.shape[2]
    src_total = own_count + node_count * slot_total
    node_total = own_count * node_count
    grad_scale = 1.0 / math.sqrt(node_total)
    outgoing = pack_rows(features, send_rows, send_count)
    arrived = lax.all_to_all(outgoing, "node", split_axis=0, concat_axis=0, tiled=True).reshape(
        -1, features.shape[1]
    )
    agg_one = aggregate(features, arrived, tile_src, tile_val)
    partial_one = jnp.dot(features, w_self1, preferred_element_type=jnp.float32)
    partial_one = partial_one + jnp.dot(agg_one, w_neigh1, preferred_element_type=jnp.float32)
    pre_act = lax.psum_scatter(partial_one, "feat", scatter_dimension=1, tiled=True)
    activated, pullback = jax.vjp(lambda inner: jax.nn.gelu(inner, approximate=True), pre_act)
    hidden = activated.astype(jnp.bfloat16)
    unit_count = hidden.shape[1]
    outgoing_two = pack_rows(hidden, send_rows, send_count)
    arrived_two = lax.all_to_all(
        outgoing_two, "node", split_axis=0, concat_axis=0, tiled=True
    ).reshape(-1, unit_count)
    agg_two = aggregate(hidden, arrived_two, tile_src, tile_val)
    partial_two = jnp.dot(hidden, w_self2, preferred_element_type=jnp.float32)
    partial_two = partial_two + jnp.dot(agg_two, w_neigh2, preferred_element_type=jnp.float32)
    logits = lax.psum(partial_two, "feat")
    row_loss, dlogits = cross_entropy(logits, labels, grad_scale)
    mean_loss = lax.psum(jnp.sum(row_loss), "node") / node_total
    grad_pair = lax.psum(
        (
            jnp.einsum("nh,nc->hc", hidden, dlogits, preferred_element_type=jnp.float32),
            jnp.einsum("nh,nc->hc", agg_two, dlogits, preferred_element_type=jnp.float32),
        ),
        "node",
    )
    back_grad = jnp.einsum(
        "nc,hc->nh", dlogits, w_neigh2, preferred_element_type=jnp.float32
    ).astype(jnp.bfloat16)
    direct = jnp.einsum("nc,hc->nh", dlogits, w_self2, preferred_element_type=jnp.float32)
    landed = spread_back(back_grad, tile_src, tile_val, src_total)
    halo_back = landed[own_count:].reshape(node_count, slot_total, unit_count)
    returned = lax.all_to_all(
        halo_back.astype(jnp.bfloat16), "node", split_axis=0, concat_axis=0, tiled=True
    ).astype(halo_back.dtype)
    in_use = jnp.arange(slot_total, dtype=jnp.int32)[None, :] < send_count[0][:, None]
    returned = jnp.where(in_use[:, :, None], returned, jnp.zeros_like(returned))
    back_rows = jax.ops.segment_sum(
        returned.reshape(-1, unit_count), send_rows[0].reshape(-1), num_segments=own_count
    )
    back_hidden = direct + landed[:own_count] + back_rows
    pre_grad = pullback(back_hidden)[0].astype(jnp.bfloat16)
    shard_piece = lax.all_gather(pre_grad, "feat", axis=1, tiled=True)
    local_grads = jnp.stack(
        [
            jnp.einsum("nf,nh->fh", features, shard_piece, preferred_element_type=jnp.float32),
            jnp.einsum("nf,nh->fh", agg_one, shard_piece, preferred_element_type=jnp.float32),
        ]
    )
    summed = lax.psum(local_grads, "node")
    return (mean_loss, summed[0], summed[1], grad_pair[0], grad_pair[1])


def solution(mesh):
    in_specs = (
        P("node", "feat"),
        P("node", None, None),
        P("node", None),
        P("node", None),
        P("node", None, None, None),
        P("node"),
        P("feat", None),
        P("feat", None),
        P("feat", None),
        P("feat", None),
    )
    out_specs = (P(), P("feat", None), P("feat", None), P("feat", None), P("feat", None))
    return jax.shard_map(shards, mesh=mesh, in_specs=in_specs, out_specs=out_specs, check_vma=False)
```

profile of v0, /device:TPU:2, one launch (start us, length us, event | category | flops | bytes accessed | tf_op | source)
XLA Modules:
  0.0 571.0 jit_solution(3139560621322994043)
XLA Ops:
  7.2 1.0 reshape_squeeze.7
  8.2 0.9 iota_compare_fusion.1
  9.1 0.9 copy.35
  10.0 12.1 %gather_fusion = bf16[4096,32]{1,0:T(8,128)(2,1)S(1)} fusion(bf16[512,32]{1,0:T(8,128)(2,1)S(1)} %copy.35, s32[4096]{0:T(1024)S(1)} %broadcast_clamp_fusion), kind=kCustom, calls=%fused_computation | custom fusion | bytes 540672 | tf_op jit(solution)/shard_map/jit(_take)/gather | solution.py:10
  22.1 1.1 copy.36
  23.3 1.2 fusion.30
  24.4 1.0 reshape.178
  25.4 12.1 %all-to-all-start = ((bf16[64,2,1024]{2,1,0:T(2,128)(2,1)}), bf16[64,2,1024]{2,1,0:T(2,128)(2,1)S(1)}, u32[]{:S(2)}, u32[]{:S(2)}) async-start(bf16[64,2,1024]{2,1,0:T(2,128)(2,1)} %reshape.178), calls=%async_computation | async-start | bytes 524288 | tf_op jit(solution)/shard_map/all_to_all | solution.py:74
  37.7 1.8 fusion.31
  39.5 10.0 %all-to-all-done = bf16[64,2,1024]{2,1,0:T(2,128)(2,1)S(1)} async-done(((bf16[64,2,1024]{2,1,0:T(2,128)(2,1)}), bf16[64,2,1024]{2,1,0:T(2,128)(2,1)S(1)}, u32[]{:S(2)}, u32[]{:S(2)}) %all-to-all-start) | async-done | bytes 262176 | tf_op jit(solution)/shard_map/all_to_all | solution.py:74
  51.3 0.8 fusion.11
  52.1 0.7 copy-done.3
  52.9 1.8 convolution_add_fusion
  54.7 28.0 %reduce-scatter.2.cloned.1.call-done = f32[512,256]{1,0:T(8,128)} async-done(((f32[512,1024]{1,0:T(8,128)}), f32[512,256]{1,0:T(8,128)}) %reduce-scatter.2.cloned.1.call-update) | async-done | bytes 524304 | tf_op jit(solution)/shard_map/reduce_scatter | solution.py:80
  82.7 1.2 multiply_convert_fusion
  83.9 16.9 %gather_fusion.2 = bf16[4096,256]{1,0:T(8,128)(2,1)} fusion(bf16[512,256]{1,0:T(8,128)(2,1)S(1)} %multiply_convert_fusion, s32[4096]{0:T(1024)S(1)} %broadcast_clamp_fusion), kind=kCustom, calls=%fused_computation.2 | custom fusion | bytes 4210688 | tf_op jit(solution)/shard_map/jit(_take)/gather | solution.py:10
  100.8 4.4 select_select_fusion
  105.2 10.9 %all-to-all-start.1 = ((bf16[64,64,256]{2,1,0:T(8,128)(2,1)}), bf16[64,64,256]{2,1,0:T(8,128)(2,1)}, u32[]{:S(2)}, u32[]{:S(2)}) async-start(bf16[64,64,256]{2,1,0:T(8,128)(2,1)} %select_select_fusion), calls=%async_computation.2 | async-start | bytes 4194304 | tf_op jit(solution)/shard_map/all_to_all | solution.py:85
  116.4 50.7 %all-to-all-done.1 = bf16[64,64,256]{2,1,0:T(8,128)(2,1)} async-done(((bf16[64,64,256]{2,1,0:T(8,128)(2,1)}), bf16[64,64,256]{2,1,0:T(8,128)(2,1)}, u32[]{:S(2)}, u32[]{:S(2)}) %all-to-all-start.1) | async-done | bytes 2097184 | tf_op jit(solution)/shard_map/all_to_all | solution.py:85
  167.1 3.2 pad_maximum_fusion
  170.3 4.4 gather_fusion.3
  174.7 3.2 fusion.7
  178.0 1.0 convolution_add_fusion.2
  179.0 42.6 %all-reduce.4.cloned.1.call-done = f32[512,172]{0,1:T(8,128)} async-done(((f32[512,172]{0,1:T(8,128)}), f32[512,172]{0,1:T(8,128)}) %all-reduce.4.cloned.1.call-update) | async-done | bytes 352272 | tf_op jit(solution)/shard_map/psum | solution.py:91
  221.7 1.0 reduce_max.9
  222.7 1.1 exponential_reduce_fusion
  223.8 1.1 multiply_convert_fusion.1
  225.2 4.5 convolution_bitcast_fusion
  229.7 8.7 %copy.41 = f32[4,16,128,256]{3,2,1,0:T(8,128)} copy(f32[4,16,128,256]{2,3,1,0:T(8,128)} %convolution_bitcast_fusion) | data formatting | bytes 16777216 | tf_op jit(solution)/shard_map/bkij,bih->bkjh/dot_general | solution.py:26
  238.4 8.1 %copy.49 = f32[8,8,128,256]{3,1,2,0:T(8,128)S(1)} copy(f32[8,8,128,256]{3,2,1,0:T(8,128)} %bitcast.90) | data formatting | bytes 16777216
  246.5 4.3 fusion.26
  250.8 2.3 copy-done.2
  253.4 2.4 convert_element_type.51
  255.9 10.9 %all-to-all-start.2 = ((bf16[64,64,256]{2,1,0:T(8,128)(2,1)}), bf16[64,64,256]{2,1,0:T(8,128)(2,1)}, u32[]{:S(2)}, u32[]{:S(2)}) async-start(bf16[64,64,256]{2,1,0:T(8,128)(2,1)} %convert_element_type.51), calls=%async_computation.3 | async-start | bytes 4194304 | tf_op jit(solution)/shard_map/all_to_all | solution.py:107
  267.5 50.3 %all-to-all-done.2 = bf16[64,64,256]{2,1,0:T(8,128)(2,1)} async-done(((bf16[64,64,256]{2,1,0:T(8,128)(2,1)}), bf16[64,64,256]{2,1,0:T(8,128)(2,1)}, u32[]{:S(2)}, u32[]{:S(2)}) %all-to-all-start.2) | async-done | bytes 2097184 | tf_op jit(solution)/shard_map/all_to_all | solution.py:107
  317.8 3.5 convert_select_fusion
  321.3 23.3 %scatter_fusion = f32[512,256]{1,0:T(8,128)S(1)} fusion(f32[512,256]{1,0:T(8,128)S(1)} %convolution_add_fusion.1, s32[4096]{0:T(1024)S(1)} %reshape.164, f32[4096,256]{1,0:T(8,128)} %bitcast.92), kind=kCustom, calls=%fused_computation.4 | custom fusion | flops 1048576 | bytes 12599296 | tf_op jit(solution)/shard_map/scatter-add | solution.py:112
  344.6 1.1 fusion.18
  345.7 0.9 fusion.34
  346.6 0.9 fusion.33
  347.5 23.0 %all-gather.2.cloned.1.call-done = bf16[512,1024]{1,0:T(8,128)(2,1)} async-done(((bf16[512,256]{1,0:T(8,128)(2,1)}), bf16[512,1024]{1,0:T(8,128)(2,1)}) %all-gather.2.cloned.1.call-update) | async-done | bytes 1048592 | tf_op jit(solution)/shard_map/all_gather | solution.py:117
  370.5 1.7 convolution_bitcast_fusion.2
  372.2 1.5 convolution_bitcast_fusion.1
  375.0 128.7 %psum.36 = f32[]{:T(128)} all-reduce(f32[]{:T(128)} %subtract_reduce_fusion), channel_id=1, replica_groups=mesh['node'=64,'feat'=4] {'node'}, use_global_device_ids=true, to_apply=%region_6.7 | all-reduce | flops 1 | bytes 8 | tf_op jit(solution)/shard_map/psum | solution.py:93
  504.4 54.0 %all-reduce.6.cloned.1.call-done = (f32[2,32,1024]{2,1,0:T(8,128)}, f32[256,172]{0,1:T(8,128)}, f32[256,172]{0,1:T(8,128)}) async-done(((f32[2,32,1024]{2,1,0:T(8,128)}, f32[256,172]{0,1:T(8,128)}, f32[256,172]{0,1:T(8,128)}), (f32[2,32,1024]{2,1,0:T(8,128)}, f32[256,172]{0,1:T(8,128)}, f32[256,172]{0,1:T(8,128)})) %all-reduce.6.cloned.1.call-update) | async-done | bytes 614416 | tf_op jit(solution)/shard_map/psum | solution.py:124
  558.4 1.7 slice_bitcast_fusion
  560.1 1.6 copy.64
  561.7 1.6 copy.65
  (54 shorter events, 5.1 us)
Async XLA Ops:
  7.2 44.1 %copy-start = (bf16[4,16,128,128]{3,2,1,0:T(8,128)(2,1)S(1)}, bf16[4,16,128,128]{3,2,1,0:T(8,128)(2,1)}, u32[]{:S(2)}) copy-start(bf16[4,16,128,128]{3,2,1,0:T(8,128)(2,1)} %param.14) | copy-start | bytes 6291460
  22.1 15.5 %copy-start.11 = (s32[4,16]{1,0:T(4,128)S(1)}, s32[4,16]{1,0:T(4,128)}, u32[]{:S(2)}) copy-start(s32[4,16]{1,0:T(4,128)} %param.13) | copy-start | bytes 772
  22.1 15.6 %copy-start.5 = (bf16[512,32]{0,1:T(8,128)(2,1)S(1)}, bf16[512,32]{0,1:T(8,128)(2,1)}, u32[]{:S(2)}) copy-start(bf16[512,32]{0,1:T(8,128)(2,1)} %param.10) | copy-start | bytes 98308
  22.1 15.6 %copy-start.10 = (bf16[32,1024]{1,0:T(8,128)(2,1)S(1)}, bf16[32,1024]{1,0:T(8,128)(2,1)}, u32[]{:S(2)}) copy-start(bf16[32,1024]{1,0:T(8,128)(2,1)} %param.16) | copy-start | bytes 196612
  25.4 24.1 %all-to-all-start = ((bf16[64,2,1024]{2,1,0:T(2,128)(2,1)}), bf16[64,2,1024]{2,1,0:T(2,128)(2,1)S(1)}, u32[]{:S(2)}, u32[]{:S(2)}) async-start(bf16[64,2,1024]{2,1,0:T(2,128)(2,1)} %reshape.178), calls=%async_computation | async-start | bytes 524288 | tf_op jit(solution)/shard_map/all_to_all | solution.py:74
  37.5 45.1 %reduce-scatter.2.cloned.1.call-start = ((), (), s32[]{:S(2)}) async-start(), calls=%async_computation.4 | async-start | bytes 2621440 | tf_op jit(solution)/shard_map/reduce_scatter | solution.py:80
  51.3 1.6 copy-start.3
  51.3 1.6 copy-start.9
  105.2 10.9 %copy-start.7 = (bf16[256,172]{0,1:T(8,128)(2,1)S(1)}, bf16[256,172]{0,1:T(8,128)(2,1)}, u32[]{:S(2)}) copy-start(bf16[256,172]{0,1:T(8,128)(2,1)} %param.18) | copy-start | bytes 264196
  105.2 61.9 %all-to-all-start.1 = ((bf16[64,64,256]{2,1,0:T(8,128)(2,1)}), bf16[64,64,256]{2,1,0:T(8,128)(2,1)}, u32[]{:S(2)}, u32[]{:S(2)}) async-start(bf16[64,64,256]{2,1,0:T(8,128)(2,1)} %select_select_fusion), calls=%async_computation.2 | async-start | bytes 4194304 | tf_op jit(solution)/shard_map/all_to_all | solution.py:85
  116.1 105.6 %all-reduce.4.cloned.1.call-start = ((), (), s32[]{:S(2)}) async-start(), calls=%async_computation.5 | async-start | bytes 720896 | tf_op jit(solution)/shard_map/psum | solution.py:91
  174.7 3.2 copy-start.6
  174.7 48.0 %copy-start.12 = (s32[512]{0:T(512)S(1)}, s32[512]{0:T(512)}, u32[]{:S(2)}) copy-start(s32[512]{0:T(512)} %param.15) | copy-start | bytes 6148
  250.8 2.3 copy-start.2
  255.9 10.9 %copy-start.8 = (s32[1,64,64]{2,1,0:T(8,128)S(1)}, s32[1,64,64]{2,1,0:T(8,128)}, u32[]{:S(2)}) copy-start(s32[1,64,64]{2,1,0:T(8,128)} %param.11) | copy-start | bytes 49156
  255.9 11.0 %slice-start = ((f32[36,32768]{1,0:T(8,128)}), f32[4,32768]{1,0:T(4,128)S(1)}, s32[]{:S(2)}) async-start(f32[36,32768]{1,0:T(8,128)} %copy-done.2), calls=%async_computation.8 | async-start | bytes 1048576 | tf_op jit(solution)/shard_map/slice | solution.py:115
  255.9 61.9 %all-to-all-start.2 = ((bf16[64,64,256]{2,1,0:T(8,128)(2,1)}), bf16[64,64,256]{2,1,0:T(8,128)(2,1)}, u32[]{:S(2)}, u32[]{:S(2)}) async-start(bf16[64,64,256]{2,1,0:T(8,128)(2,1)} %convert_element_type.51), calls=%async_computation.3 | async-start | bytes 4194304 | tf_op jit(solution)/shard_map/all_to_all | solution.py:107
  266.7 103.8 %all-gather.2.cloned.1.call-start = ((), (), s32[]{:S(2)}) async-start(), calls=%async_computation.6 | async-start | bytes 1310720 | tf_op jit(solution)/shard_map/all_gather | solution.py:117
  321.3 23.3 %copy-start.4 = (f32[512,256]{1,0:T(8,128)S(1)}, f32[512,256]{1,0:T(8,128)}, u32[]{:S(2)}) copy-start(f32[512,256]{1,0:T(8,128)} %reduce-scatter.2.cloned.1.call-done) | copy-start | bytes 1572868
  345.7 212.8 %all-reduce.6.cloned.1.call-start = ((), (), s32[]{:S(2)}) async-start(), calls=%async_computation.7 | async-start | bytes 1245184 | tf_op jit(solution)/shard_map/psum | solution.py:124
  370.5 192.8 %copy-start.1 = (bf16[4,16,128,128]{3,2,1,0:T(8,128)(2,1)S(1)}, bf16[4,16,128,128]{3,2,1,0:T(8,128)(2,1)}, u32[]{:S(2)}) copy-start(bf16[4,16,128,128]{3,2,1,0:T(8,128)(2,1)} %param.14) | copy-start | bytes 6291460
Sparse Core Ops, SparseCore 0:
  54.8 27.8 reduce-scatter.1
  179.1 42.5 all-reduce.3
  345.8 24.6 all-gather.1
  375.2 183.2 all-reduce.5
where the time goes:
time: 572 us; the launch traced here: 571 us
  waiting for transfers between devices  259 us (45%)
  blocking collectives  129 us (23%)
  local copies, waits for them, and re-layouts  67.3 us (12%)
  other arithmetic  43.3 us (8%)
  starting transfers between devices  34 us (6%)
  matrix products  23.1 us (4%)
  between operations  15.8 us (3%)
    psum x1, blocking collectives, shards(): mean_loss = lax.psum(jnp.sum(row_loss), 'node') / node_total  129 us
    psum x1, waiting for transfers between devices, shards(): summed = lax.psum(local_grads, 'node')  54 us
    all_to_all x1, waiting for transfers between devices, shards(): lax.all_to_all(outgoing_two, 'node', split_axis=0, concat_axis=0, tiled=T...  50.7 us
    all_to_all x1, waiting for transfers between devices, shards(): lax.all_to_all(halo_back.astype(jnp.bfloat16), 'node', split_axis=0, conc...  50.3 us
    psum x1, waiting for transfers between devices, shards(): logits = lax.psum(partial_two, 'feat')  42.6 us
    gather x3, local copies, waits for them, and re-layouts, pack_rows(): picked = jnp.take(own_rows, send_rows[0].reshape(-1), axis=0)  30.2 us
    reduce_scatter x1, waiting for transfers between devices, shards(): lax.psum_scatter(partial_one, 'feat', scatter_dimension=1, tiled=True)  28 us
    scatter-add x1, other arithmetic, shards(): jax.ops.segment_sum(returned.reshape(-1, unit_count), send_rows[0].reshap...  23.3 us
  transfers between devices with their start and end apart: 7, of which 7 were waited for; matrix products, arithmetic and copies ran while one was open for 1% of the time, Pallas kernels for 0%

commit v1 on v0

--- a/solution.py
+++ b/solution.py
@@ -3,6 +3,11 @@
 import jax.numpy as jnp
 from jax import lax
 from jax.sharding import PartitionSpec as P
+
+
+def gather_by_exchange(x, axis, dim):
+    copies = jnp.concatenate([x] * lax.axis_size(axis), axis=dim)
+    return lax.all_to_all(copies, axis, dim, dim, tiled=True)
 
 
 def pack_rows(own_rows, send_rows, send_count):
@@ -114,7 +119,7 @@
     )
     back_hidden = direct + landed[:own_count] + back_rows
     pre_grad = pullback(back_hidden)[0].astype(jnp.bfloat16)
-    shard_piece = lax.all_gather(pre_grad, "feat", axis=1, tiled=True)
+    shard_piece = gather_by_exchange(pre_grad, "feat", 1)
     local_grads = jnp.stack(
         [
             jnp.einsum("nf,nh->fh", features, shard_piece, preferred_element_type=jnp.float32),

time: 572 us -> 559 us (0.977)
  waiting for transfers between devices: 259 us -> 245 us
    all_gather x1 -> x0, waiting for transfers between devices: 23 us -> none  [shards(): shard_piece = lax.all_gather(pre_grad, 'feat', axis=1, tiled=True)]
    all_to_all x0 -> x1, waiting for transfers between devices: none -> 12.4 us  [gather_by_exchange(): return lax.all_to_all(copies, axis, dim, dim, tiled=True)]
where the time goes in v1:
time: 559 us; the launch traced here: 557 us
  waiting for transfers between devices  245 us (44%)
  blocking collectives  125 us (22%)
  local copies, waits for them, and re-layouts  69 us (12%)
  other arithmetic  42.7 us (8%)
  starting transfers between devices  38.9 us (7%)
  matrix products  20.7 us (4%)
  between operations  15.9 us (3%)
    psum x1, blocking collectives, shards(): mean_loss = lax.psum(jnp.sum(row_loss), 'node') / node_total  125 us
    psum x1, waiting for transfers between devices, shards(): summed = lax.psum(local_grads, 'node')  51.2 us
    all_to_all x1, waiting for transfers between devices, shards(): lax.all_to_all(outgoing_two, 'node', split_axis=0, concat_axis=0, tiled=T...  50.7 us
    all_to_all x1, waiting for transfers between devices, shards(): lax.all_to_all(halo_back.astype(jnp.bfloat16), 'node', split_axis=0, conc...  50.3 us
    psum x1, waiting for transfers between devices, shards(): logits = lax.psum(partial_two, 'feat')  42.6 us
    gather x3, local copies, waits for them, and re-layouts, pack_rows(): picked = jnp.take(own_rows, send_rows[0].reshape(-1), axis=0)  30.3 us
    reduce_scatter x1, waiting for transfers between devices, shards(): lax.psum_scatter(partial_one, 'feat', scatter_dimension=1, tiled=True)  28 us
    scatter-add x1, other arithmetic, shards(): jax.ops.segment_sum(returned.reshape(-1, unit_count), send_rows[0].reshap...  23.3 us
  transfers between devices with their start and end apart: 7, of which 7 were waited for; matrix products, arithmetic and copies ran while one was open for 1% of the time, Pallas kernels for 0%

profile of v1, /device:TPU:2, one launch (start us, length us, event | category | flops | bytes accessed | tf_op | source)
XLA Modules:
  0.0 557.4 jit_solution(8991511715885218254)
XLA Ops:
  7.2 1.0 reshape_squeeze.7
  8.2 0.9 iota_compare_fusion.1
  9.1 0.9 copy.36
  10.0 12.1 %gather_fusion = bf16[4096,32]{1,0:T(8,128)(2,1)S(1)} fusion(bf16[512,32]{1,0:T(8,128)(2,1)S(1)} %copy.36, s32[4096]{0:T(1024)S(1)} %broadcast_clamp_fusion), kind=kCustom, calls=%fused_computation | custom fusion | bytes 540672 | tf_op jit(solution)/shard_map/jit(_take)/gather | solution.py:15
  22.1 1.1 copy.37
  23.3 1.2 fusion.30
  24.4 1.0 reshape.181
  25.4 12.1 %all-to-all-start = ((bf16[64,2,1024]{2,1,0:T(2,128)(2,1)}), bf16[64,2,1024]{2,1,0:T(2,128)(2,1)S(1)}, u32[]{:S(2)}, u32[]{:S(2)}) async-start(bf16[64,2,1024]{2,1,0:T(2,128)(2,1)} %reshape.181), calls=%async_computation | async-start | bytes 524288 | tf_op jit(solution)/shard_map/all_to_all | solution.py:79
  37.7 1.8 fusion.31
  39.5 10.0 %all-to-all-done = bf16[64,2,1024]{2,1,0:T(2,128)(2,1)S(1)} async-done(((bf16[64,2,1024]{2,1,0:T(2,128)(2,1)}), bf16[64,2,1024]{2,1,0:T(2,128)(2,1)S(1)}, u32[]{:S(2)}, u32[]{:S(2)}) %all-to-all-start) | async-done | bytes 262176 | tf_op jit(solution)/shard_map/all_to_all | solution.py:79
  51.3 0.8 fusion.11
  52.1 0.7 copy-done.3
  52.9 1.8 convolution_add_fusion
  54.7 28.0 %reduce-scatter.2.cloned.1.call-done = f32[512,256]{1,0:T(8,128)} async-done(((f32[512,1024]{1,0:T(8,128)}), f32[512,256]{1,0:T(8,128)}) %reduce-scatter.2.cloned.1.call-update) | async-done | bytes 524304 | tf_op jit(solution)/shard_map/reduce_scatter | solution.py:85
  82.7 1.2 multiply_convert_fusion
  83.9 17.0 %gather_fusion.2 = bf16[4096,256]{1,0:T(8,128)(2,1)} fusion(bf16[512,256]{1,0:T(8,128)(2,1)S(1)} %multiply_convert_fusion, s32[4096]{0:T(1024)S(1)} %broadcast_clamp_fusion), kind=kCustom, calls=%fused_computation.2 | custom fusion | bytes 4210688 | tf_op jit(solution)/shard_map/jit(_take)/gather | solution.py:15
  101.0 4.4 select_select_fusion
  105.3 10.8 %all-to-all-start.1 = ((bf16[64,64,256]{2,1,0:T(8,128)(2,1)}), bf16[64,64,256]{2,1,0:T(8,128)(2,1)}, u32[]{:S(2)}, u32[]{:S(2)}) async-start(bf16[64,64,256]{2,1,0:T(8,128)(2,1)} %select_select_fusion), calls=%async_computation.2 | async-start | bytes 4194304 | tf_op jit(solution)/shard_map/all_to_all | solution.py:90
  116.5 50.7 %all-to-all-done.1 = bf16[64,64,256]{2,1,0:T(8,128)(2,1)} async-done(((bf16[64,64,256]{2,1,0:T(8,128)(2,1)}), bf16[64,64,256]{2,1,0:T(8,128)(2,1)}, u32[]{:S(2)}, u32[]{:S(2)}) %all-to-all-start.1) | async-done | bytes 2097184 | tf_op jit(solution)/shard_map/all_to_all | solution.py:90
  167.2 3.2 pad_maximum_fusion
  170.4 4.4 gather_fusion.3
  174.8 3.2 fusion.7
  178.1 1.0 convolution_add_fusion.2
  179.2 42.6 %all-reduce.4.cloned.1.call-done = f32[512,172]{0,1:T(8,128)} async-done(((f32[512,172]{0,1:T(8,128)}), f32[512,172]{0,1:T(8,128)}) %all-reduce.4.cloned.1.call-update) | async-done | bytes 352272 | tf_op jit(solution)/shard_map/psum | solution.py:96
  221.8 1.0 reduce_max.9
  222.8 1.1 exponential_reduce_fusion
  223.9 1.1 multiply_convert_fusion.1
  225.3 4.5 convolution_bitcast_fusion
  229.8 8.7 %copy.42 = f32[4,16,128,256]{3,2,1,0:T(8,128)} copy(f32[4,16,128,256]{2,3,1,0:T(8,128)} %convolution_bitcast_fusion) | data formatting | bytes 16777216 | tf_op jit(solution)/shard_map/bkij,bih->bkjh/dot_general | solution.py:31
  238.5 8.1 %copy.53 = f32[8,8,128,256]{3,1,2,0:T(8,128)S(1)} copy(f32[8,8,128,256]{3,2,1,0:T(8,128)} %bitcast.95) | data formatting | bytes 16777216
  246.6 4.3 fusion.26
  250.9 2.3 copy-done.2
  253.6 2.5 convert_element_type.53
  256.0 10.9 %all-to-all-start.2 = ((bf16[64,64,256]{2,1,0:T(8,128)(2,1)}), bf16[64,64,256]{2,1,0:T(8,128)(2,1)}, u32[]{:S(2)}, u32[]{:S(2)}) async-start(bf16[64,64,256]{2,1,0:T(8,128)(2,1)} %convert_element_type.53), calls=%async_computation.3 | async-start | bytes 4194304 | tf_op jit(solution)/shard_map/all_to_all | solution.py:112
  267.6 50.3 %all-to-all-done.2 = bf16[64,64,256]{2,1,0:T(8,128)(2,1)} async-done(((bf16[64,64,256]{2,1,0:T(8,128)(2,1)}), bf16[64,64,256]{2,1,0:T(8,128)(2,1)}, u32[]{:S(2)}, u32[]{:S(2)}) %all-to-all-start.2) | async-done | bytes 2097184 | tf_op jit(solution)/shard_map/all_to_all | solution.py:112
  317.9 3.5 convert_select_fusion
  321.5 23.3 %scatter_fusion = f32[512,256]{1,0:T(8,128)S(1)} fusion(f32[512,256]{1,0:T(8,128)S(1)} %convolution_add_fusion.1, s32[4096]{0:T(1024)S(1)} %reshape.167, f32[4096,256]{1,0:T(8,128)} %bitcast.97), kind=kCustom, calls=%fused_computation.4 | custom fusion | flops 1048576 | bytes 12599296 | tf_op jit(solution)/shard_map/scatter-add | solution.py:117
  345.2 1.0 copy.64
  346.3 5.0 all-to-all-start.3
  351.3 0.9 fusion.34
  352.2 0.9 fusion.33
  353.1 12.4 %all-to-all-done.3 = bf16[512,4,256]{2,0,1:T(8,128)(2,1)S(1)} async-done(((bf16[512,4,256]{2,0,1:T(8,128)(2,1)}), bf16[512,4,256]{2,0,1:T(8,128)(2,1)S(1)}, u32[]{:S(2)}, u32[]{:S(2)}) %all-to-all-start.3) | async-done | bytes 1048608 | tf_op jit(solution)/shard_map/all_to_all | solution.py:10
  366.9 0.7 pad_maximum_fusion.2
  368.2 124.8 %psum.36 = f32[]{:T(128)} all-reduce(f32[]{:T(128)} %subtract_reduce_fusion), channel_id=1, replica_groups=mesh['node'=64,'feat'=4] {'node'}, use_global_device_ids=true, to_apply=%region_6.7 | all-reduce | flops 1 | bytes 8 | tf_op jit(solution)/shard_map/psum | solution.py:98
  493.6 51.2 %all-reduce.6.cloned.1.call-done = (f32[2,32,1024]{2,1,0:T(8,128)}, f32[256,172]{0,1:T(8,128)}, f32[256,172]{0,1:T(8,128)}) async-done(((f32[2,32,1024]{2,1,0:T(8,128)}, f32[256,172]{0,1:T(8,128)}, f32[256,172]{0,1:T(8,128)}), (f32[2,32,1024]{2,1,0:T(8,128)}, f32[256,172]{0,1:T(8,128)}, f32[256,172]{0,1:T(8,128)})) %all-reduce.6.cloned.1.call-update) | async-done | bytes 614416 | tf_op jit(solution)/shard_map/psum | solution.py:129
  544.9 1.7 slice_bitcast_fusion
  546.6 1.6 copy.70
  548.2 1.6 copy.71
  (56 shorter events, 6.0 us)
Async XLA Ops:
  7.2 44.1 %copy-start = (bf16[4,16,128,128]{3,2,1,0:T(8,128)(2,1)S(1)}, bf16[4,16,128,128]{3,2,1,0:T(8,128)(2,1)}, u32[]{:S(2)}) copy-start(bf16[4,16,128,128]{3,2,1,0:T(8,128)(2,1)} %param.14) | copy-start | bytes 6291460
  22.1 15.5 %copy-start.11 = (s32[4,16]{1,0:T(4,128)S(1)}, s32[4,16]{1,0:T(4,128)}, u32[]{:S(2)}) copy-start(s32[4,16]{1,0:T(4,128)} %param.13) | copy-start | bytes 772
  22.1 15.6 %copy-start.5 = (bf16[512,32]{0,1:T(8,128)(2,1)S(1)}, bf16[512,32]{0,1:T(8,128)(2,1)}, u32[]{:S(2)}) copy-start(bf16[512,32]{0,1:T(8,128)(2,1)} %param.10) | copy-start | bytes 98308
  22.1 15.6 %copy-start.10 = (bf16[32,1024]{1,0:T(8,128)(2,1)S(1)}, bf16[32,1024]{1,0:T(8,128)(2,1)}, u32[]{:S(2)}) copy-start(bf16[32,1024]{1,0:T(8,128)(2,1)} %param.16) | copy-start | bytes 196612
  25.4 24.1 %all-to-all-start = ((bf16[64,2,1024]{2,1,0:T(2,128)(2,1)}), bf16[64,2,1024]{2,1,0:T(2,128)(2,1)S(1)}, u32[]{:S(2)}, u32[]{:S(2)}) async-start(bf16[64,2,1024]{2,1,0:T(2,128)(2,1)} %reshape.181), calls=%async_computation | async-start | bytes 524288 | tf_op jit(solution)/shard_map/all_to_all | solution.py:79
  37.6 45.2 %reduce-scatter.2.cloned.1.call-start = ((), (), s32[]{:S(2)}) async-start(), calls=%async_computation.5 | async-start | bytes 2621440 | tf_op jit(solution)/shard_map/reduce_scatter | solution.py:85
  51.3 1.6 copy-start.3
  51.3 1.6 copy-start.9
  105.3 10.9 %copy-start.7 = (bf16[256,172]{0,1:T(8,128)(2,1)S(1)}, bf16[256,172]{0,1:T(8,128)(2,1)}, u32[]{:S(2)}) copy-start(bf16[256,172]{0,1:T(8,128)(2,1)} %param.18) | copy-start | bytes 264196
  105.3 61.9 %all-to-all-start.1 = ((bf16[64,64,256]{2,1,0:T(8,128)(2,1)}), bf16[64,64,256]{2,1,0:T(8,128)(2,1)}, u32[]{:S(2)}, u32[]{:S(2)}) async-start(bf16[64,64,256]{2,1,0:T(8,128)(2,1)} %select_select_fusion), calls=%async_computation.2 | async-start | bytes 4194304 | tf_op jit(solution)/shard_map/all_to_all | solution.py:90
  116.2 105.6 %all-reduce.4.cloned.1.call-start = ((), (), s32[]{:S(2)}) async-start(), calls=%async_computation.6 | async-start | bytes 720896 | tf_op jit(solution)/shard_map/psum | solution.py:96
  174.8 3.2 copy-start.6
  174.8 48.0 %copy-start.12 = (s32[512]{0:T(512)S(1)}, s32[512]{0:T(512)}, u32[]{:S(2)}) copy-start(s32[512]{0:T(512)} %param.15) | copy-start | bytes 6148
  250.9 2.3 copy-start.2
  256.0 10.9 %copy-start.8 = (s32[1,64,64]{2,1,0:T(8,128)S(1)}, s32[1,64,64]{2,1,0:T(8,128)}, u32[]{:S(2)}) copy-start(s32[1,64,64]{2,1,0:T(8,128)} %param.11) | copy-start | bytes 49156
  256.0 11.0 %slice-start = ((f32[36,32768]{1,0:T(8,128)}), f32[4,32768]{1,0:T(4,128)S(1)}, s32[]{:S(2)}) async-start(f32[36,32768]{1,0:T(8,128)} %copy-done.2), calls=%async_computation.8 | async-start | bytes 1048576 | tf_op jit(solution)/shard_map/slice | solution.py:120
  256.0 61.9 %all-to-all-start.2 = ((bf16[64,64,256]{2,1,0:T(8,128)(2,1)}), bf16[64,64,256]{2,1,0:T(8,128)(2,1)}, u32[]{:S(2)}, u32[]{:S(2)}) async-start(bf16[64,64,256]{2,1,0:T(8,128)(2,1)} %convert_element_type.53), calls=%async_computation.3 | async-start | bytes 4194304 | tf_op jit(solution)/shard_map/all_to_all | solution.py:112
  321.5 23.3 %copy-start.4 = (f32[512,256]{1,0:T(8,128)S(1)}, f32[512,256]{1,0:T(8,128)}, u32[]{:S(2)}) copy-start(f32[512,256]{1,0:T(8,128)} %reduce-scatter.2.cloned.1.call-done) | copy-start | bytes 1572868
  346.3 19.2 %all-to-all-start.3 = ((bf16[512,4,256]{2,0,1:T(8,128)(2,1)}), bf16[512,4,256]{2,0,1:T(8,128)(2,1)S(1)}, u32[]{:S(2)}, u32[]{:S(2)}) async-start(bf16[512,4,256]{2,0,1:T(8,128)(2,1)} %bitcast.93), calls=%async_computation.4 | async-start | bytes 2097152 | tf_op jit(solution)/shard_map/all_to_all | solution.py:10
  351.3 193.6 %all-reduce.6.cloned.1.call-start = ((), (), s32[]{:S(2)}) async-start(), calls=%async_computation.7 | async-start | bytes 1245184 | tf_op jit(solution)/shard_map/psum | solution.py:129
  366.0 183.7 %copy-start.1 = (bf16[4,16,128,128]{3,2,1,0:T(8,128)(2,1)S(1)}, bf16[4,16,128,128]{3,2,1,0:T(8,128)(2,1)}, u32[]{:S(2)}) copy-start(bf16[4,16,128,128]{3,2,1,0:T(8,128)(2,1)} %param.14) | copy-start | bytes 6291460
Sparse Core Ops, SparseCore 0:
  54.8 27.8 reduce-scatter.1
  179.2 42.5 all-reduce.3
  367.8 177.0 all-reduce.5
